TPU v7x, 256 devices: a whole 4x4x8 slice. The times are simulated.
256 devices in a mesh: dp: 32 (over z, y), grp: 8 (over x, core).
Axes of the slice: x: 4, y: 4, z: 8, core: 2. Of those that a mesh axis runs over, the one named last changes fastest.
Arguments:
- tokens: bfloat16 [1024, 256, 1024], P(('dp', 'grp')), may hold values from -0.1875 to 0.1875
- patches: bfloat16 [1024, 256, 1024], P(('dp', 'grp')), may hold values from -0.1875 to 0.1875
- lengths: int32 [1024], P(('dp', 'grp')), may hold values from 16 to 256, as said below
- img_pooled: bfloat16 [1024, 1024], P(('dp', 'grp')), may hold values from -1 to 1
- txt_pooled: bfloat16 [1024, 1024], P(('dp', 'grp')), may hold values from -1 to 1
Outputs:
- grad_tokens: bfloat16 [1024, 256, 1024], P(('dp', 'grp'))
- grad_patches: bfloat16 [1024, 256, 1024], P(('dp', 'grp'))
- grad_img: bfloat16 [1024, 1024], P(('dp', 'grp'))
- grad_txt: bfloat16 [1024, 1024], P(('dp', 'grp'))
- loss_mean: float32 [], replicated
Inputs may be any that keep to these rules, and one draw needn't show every extreme that they name: `lengths`: among the pairs of one index of dp (8 devices along grp), exactly 8 captions have more than 128 tokens; no device holds more than two of them and some device holds two; some caption has exactly 256 tokens and some exactly 128.
All inputs are finite; a program needn't handle non-finite values.
Results may differ from a plain program's by a relative error of at most 0.013.
Values may be sent and summed in bfloat16 or wider, within the bound.
A program may use at most 128 MiB of HBM per device.

v0:
```python
import jax
import jax.numpy as jnp
from jax import lax
from jax.sharding import Mesh
from jax.sharding import PartitionSpec as P

DP_GRP = ("dp_0", "dp_1", "grp_0", "grp_1")


RANGE_EPS = 1e-06
NORM_EPS = 1e-06
GLOBAL_SCALE = 100.0
FINE_SCALE = 50.0
MASK_FILL = -1000000000.0


def side_by_side(arrays, axis, dim, along):
    ends, at = ([], 0)
    for a in arrays[:-1]:
        at += a.shape[along]
        ends.append(at)
    both = jnp.concatenate(arrays, axis=along)
    return tuple(jnp.split(lax.all_gather(both, axis, axis=dim, tiled=True), ends, axis=along))


def gather_turned(arrays, axis, dims):
    turned = [jnp.moveaxis(a, dim, 0) for a, dim in zip(arrays, dims)]
    both = jnp.concatenate([t.reshape(len(t), -1) for t in turned], axis=1)
    filled, at, gathered = (lax.all_gather(both, axis, axis=0, tiled=True), 0, [])
    for t, dim in zip(turned, dims):
        section = filled[:, at : at + t[0].size].reshape(-1, *t.shape[1:])
        gathered.append(jnp.moveaxis(section, 0, dim))
        at += t[0].size
    return tuple(gathered)


def over_axes(array, axes):
    for axis in axes:
        array = lax.psum(array, axis)
    return array


def pair_terms(tok_rows, patch_rows, length):
    patch_count = patch_rows.shape[0]
    slot_count = tok_rows.shape[0]
    similar = jnp.dot(tok_rows, patch_rows.T, preferred_element_type=jnp.float32)
    lowest = jnp.min(similar, 1, keepdims=True)
    highest = jnp.max(similar, 1, keepdims=True)
    scaled = (similar - lowest) / (highest - lowest + RANGE_EPS)
    weights = jnp.maximum(scaled - 1.0 / patch_count, 0.0)
    weights = weights / jnp.sum(weights, 1, keepdims=True)
    grouped = jnp.dot(weights.astype(jnp.bfloat16), patch_rows, preferred_element_type=jnp.float32)
    group_unit = grouped * lax.rsqrt(jnp.sum(grouped * grouped, 1, keepdims=True) + NORM_EPS)
    token_float = tok_rows.astype(jnp.float32)
    token_unit = token_float * lax.rsqrt(
        jnp.sum(token_float * token_float, 1, keepdims=True) + NORM_EPS
    )
    logits = FINE_SCALE * jnp.dot(
        group_unit.astype(jnp.bfloat16),
        token_unit.astype(jnp.bfloat16).T,
        preferred_element_type=jnp.float32,
    )
    position = jnp.arange(slot_count, dtype=jnp.int32)
    valid = position < length
    both_valid = jnp.logical_and(valid[:, None], valid[None, :])
    masked = jnp.where(both_valid, logits, MASK_FILL)
    row_lse = jax.nn.logsumexp(masked, 1)
    col_lse = jax.nn.logsumexp(masked, 0)
    per_token = jnp.where(valid, row_lse + col_lse - 2.0 * jnp.diagonal(logits), 0.0)
    return jnp.sum(per_token) / (2.0 * length.astype(jnp.float32))


def pair_grads(tok_rows, patch_rows, length):

    def closure(first_arg, second_arg):
        return pair_terms(first_arg, second_arg, length)

    value, pullback = jax.vjp(closure, tok_rows, patch_rows)
    grad_tok, grad_patch = pullback(jnp.ones((), jnp.float32))
    return (value, grad_tok, grad_patch)


def fine_block(tok_rows, patch_rows, length_rows):
    return jax.vmap(pair_grads)(tok_rows, patch_rows, length_rows)


def unit_rows(pooled):
    values = pooled.astype(jnp.float32)
    inverse = lax.rsqrt(jnp.sum(values * values, -1, keepdims=True) + NORM_EPS)
    return (values * inverse, inverse)


def body(tokens, patches, lengths, img_pooled, txt_pooled):
    img_unit, img_inverse = unit_rows(img_pooled)
    txt_unit, txt_inverse = unit_rows(txt_pooled)
    img_half = img_unit.astype(jnp.bfloat16)
    txt_half = txt_unit.astype(jnp.bfloat16)
    all_img, all_txt = side_by_side((img_half, txt_half), DP_GRP, 0, 1)
    local_pairs = img_half.shape[0]
    pair_total = all_img.shape[0]
    offset = lax.axis_index(DP_GRP) * local_pairs
    own_mask = (
        jnp.arange(pair_total, dtype=jnp.int32)[None, :]
        == offset + jnp.arange(local_pairs, dtype=jnp.int32)[:, None]
    ).astype(jnp.float32)
    row_logits = GLOBAL_SCALE * jnp.dot(img_half, all_txt.T, preferred_element_type=jnp.float32)
    col_logits = GLOBAL_SCALE * jnp.dot(txt_half, all_img.T, preferred_element_type=jnp.float32)
    row_lse = jax.nn.logsumexp(row_logits, 1)
    col_lse = jax.nn.logsumexp(col_logits, 1)
    matches = GLOBAL_SCALE * jnp.sum(
        img_half.astype(jnp.float32) * txt_half.astype(jnp.float32), -1
    )
    global_part = 0.5 * jnp.sum(row_lse + col_lse - 2.0 * matches)
    row_own = (0.5 * jnp.exp(row_logits - row_lse[:, None]) - 0.5 * own_mask).astype(jnp.bfloat16)
    col_own = (0.5 * jnp.exp(col_logits - col_lse[:, None]) - 0.5 * own_mask).astype(jnp.bfloat16)
    img_local = jnp.dot(row_own, all_txt, preferred_element_type=jnp.float32)
    txt_local = jnp.dot(col_own, all_img, preferred_element_type=jnp.float32)
    lse_rows, lse_cols = gather_turned((row_lse, col_lse), DP_GRP, (0, 0))
    col_rows = (0.5 * jnp.exp(row_logits - lse_cols[None, :]) - 0.5 * own_mask).astype(jnp.bfloat16)
    row_cols = (0.5 * jnp.exp(col_logits - lse_rows[None, :]) - 0.5 * own_mask).astype(jnp.bfloat16)
    img_dir = GLOBAL_SCALE * (
        img_local + jnp.dot(col_rows, all_txt, preferred_element_type=jnp.float32)
    )
    txt_dir = GLOBAL_SCALE * (
        txt_local + jnp.dot(row_cols, all_img, preferred_element_type=jnp.float32)
    )
    grad_img = (
        (img_dir - img_unit * jnp.sum(img_unit * img_dir, -1, keepdims=True)) * img_inverse
    ).astype(jnp.bfloat16)
    grad_txt = (
        (txt_dir - txt_unit * jnp.sum(txt_unit * txt_dir, -1, keepdims=True)) * txt_inverse
    ).astype(jnp.bfloat16)
    values, grad_tokens, grad_patches = fine_block(tokens, patches, lengths)
    summed_loss = over_axes(global_part + jnp.sum(values), DP_GRP)
    loss_mean = summed_loss / pair_total
    return (grad_tokens, grad_patches, grad_img, grad_txt, loss_mean)


def solution(mesh):
    finer = Mesh(mesh.devices.reshape(8, 4, 4, 2), ("dp_0", "dp_1", "grp_0", "grp_1"))
    placed = (
        P(DP_GRP, None, None),
        P(DP_GRP, None, None),
        P(DP_GRP),
        P(DP_GRP, None),
        P(DP_GRP, None),
    )
    return jax.shard_map(
        body,
        mesh=finer,
        in_specs=placed,
        out_specs=(
            P(DP_GRP, None, None),
            P(DP_GRP, None, None),
            P(DP_GRP, None),
            P(DP_GRP, None),
            P(),
        ),
        check_vma=False,
    )
```

profile of v0, /device:TPU:1, one launch (start us, length us, event | category | flops | bytes accessed | tf_op | source)
XLA Modules:
  0.0 264.1 jit_solution(3292715968489793611)
XLA Ops:
  7.2 1.0 fusion.82
  8.2 0.8 fusion.77
  9.0 0.9 multiply_reduce_fusion.2
  9.9 0.6 maximum_bitcast_fusion
  10.6 2.1 fusion.2
  12.7 2.4 fusion.133
  15.1 0.2 maximum_reduce_fusion
  15.3 0.9 multiply_reduce_fusion
  16.3 1.9 copy-done.1
  18.2 2.0 fusion.58
  20.2 16.5 %copy.71 = f32[4,256,256]{0,2,1:T(8,128)} copy(f32[4,256,256]{1,2,0:T(8,128)S(1)} %get-tuple-element.46) | data formatting | bytes 2097152 | tf_op jit(solution)/shard_map/vmap(jvp())/mul | solution.py:58
  36.7 2.3 gather_fusion
  39.1 0.5 fusion.55
  39.7 0.3 fusion.56
  40.0 0.2 fusion.110
  40.2 1.4 and_select_fusion
  41.7 17.4 %copy.65 = f32[4,256,256]{0,2,1:T(8,128)} copy(f32[4,256,256]{1,2,0:T(8,128)} %and_select_fusion) | data formatting | bytes 2097152 | tf_op jit(solution)/shard_map/vmap(transpose(jvp(jit(_where))))/select_n | solution.py:66
  59.1 0.1 copy.66
  59.2 26.1 %scatter_fusion = f32[4,256,256]{0,2,1:T(8,128)} fusion(f32[4,256,256]{0,2,1:T(8,128)} %copy.65, s32[256]{0:T(256)S(1)} %bitcast.34, f32[256,4]{1,0:T(8,128)S(1)} %copy.66), kind=kCustom, calls=%fused_computation.1 | custom fusion | flops 1024 | bytes 14336 | tf_op jit(solution)/shard_map/vmap(transpose(jvp(jit(diagonal))))/cond/branch_0_fun/scatter-add | solution.py:69
  85.3 19.1 %copy.67 = f32[4,256,256]{1,2,0:T(8,128)S(1)} copy(f32[4,256,256]{0,2,1:T(8,128)} %scatter_fusion) | data formatting | bytes 2097152 | tf_op jit(solution)/shard_map/vmap(transpose(jvp(jit(diagonal))))/cond/branch_0_fun/scatter-add | solution.py:69
  104.4 4.3 %fusion = (f32[4,256]{1,0:T(4,128)S(1)}, bf16[4,256,1024]{2,1,0:T(8,128)(2,1)S(1)}) fusion(f32[4,256,1024]{2,1,0:T(8,128)} %copy-done.1, bf16[4,256,1024]{2,1,0:T(8,128)(2,1)} %param.5, f32[4,256]{1,0:T(4,128)S(1)} %get-tuple-element.61, f32[4,256,256]{1,2,0:T(8,128)S(1)} %copy.67), kind=kOutput, calls=%fused_computation.11 | convolution fusion | flops 544472064 | bytes 9445376 | tf_op jit(solution)/shard_map/vmap(transpose(jvp()))/dot_general | solution.py:58
  108.7 0.3 copy-done.7
  109.0 2.2 fusion.52
  111.2 0.6 divide_reduce_fusion
  111.8 4.3 %fusion.4 = (f32[4,256]{1,0:T(4,128)S(1)}, bf16[4,256,1024]{2,1,0:T(8,128)(2,1)S(1)}) fusion(bf16[4,256,1024]{2,1,0:T(8,128)(2,1)} %param.5, f32[4,256,1024]{2,1,0:T(8,128)} %copy-done.1, f32[4,256]{1,0:T(4,128)S(1)} %get-tuple-element.62, f32[4,256,256]{1,2,0:T(8,128)S(1)} %copy.67), kind=kOutput, calls=%fused_computation.15 | convolution fusion | flops 544472064 | bytes 9445376 | tf_op jit(solution)/shard_map/vmap(transpose(jvp()))/dot_general | solution.py:58
  116.1 1.0 fusion.131
  117.3 1.6 fusion.5
  118.9 2.1 convert_add_fusion
  121.0 2.6 fusion.7
  123.7 7.9 %all-gather.4.cloned.1.call-done = bf16[256,4,2048]{2,1,0:T(4,128)(2,1)} async-done(((bf16[1,4,2048]{2,1,0:T(4,128)(2,1)}), bf16[256,4,2048]{2,1,0:T(4,128)(2,1)}) %all-gather.4.cloned.1.call-update) | async-done | bytes 4194320 | tf_op jit(solution)/shard_map/all_gather | solution.py:23
  131.5 6.9 %reshape.209 = bf16[1024,2048]{1,0:T(8,128)(2,1)} reshape(bf16[256,4,2048]{2,1,0:T(4,128)(2,1)} %all-gather.4.cloned.1.call-done) | data formatting | bytes 8388608
  138.4 2.3 fusion.141
  140.8 2.4 fusion.140
  143.2 0.2 exponential_reduce_fusion
  143.4 0.2 exponential_reduce_fusion.1
  143.6 60.9 %all-gather.1 = f32[256,4,2]{1,2,0:T(2,128)S(1)} all-gather(f32[1,4,2]{1,2,0:T(2,128)S(1)} %maximum_bitcast_fusion.1), channel_id=1, replica_groups=mesh['dp_0'=8,'dp_1'=4,'grp_0'=4,'grp_1'=2] {'dp_0','dp_1','grp_0','grp_1'}, dimensions={0}, use_global_device_ids=true | all-gather | bytes 8224 | tf_op jit(solution)/shard_map/all_gather | solution.py:29
  204.5 0.6 subtract_reduce_fusion
  206.5 12.9 %psum.28 = f32[]{:T(128)} all-reduce(f32[]{:T(128)S(6)} %add.150), channel_id=1, replica_groups=mesh['dp_0'=8,'dp_1'=4,'grp_0'=4,'grp_1'=2] {'dp_0'}, use_global_device_ids=true, to_apply=%region_29.30 | all-reduce | flops 1 | bytes 8 | tf_op jit(solution)/shard_map/psum | solution.py:39
  219.3 0.2 reshape.211
  219.5 7.9 %psum.29 = f32[]{:T(128)} all-reduce(f32[]{:T(128)} %psum.28), channel_id=1, replica_groups=mesh['dp_0'=8,'dp_1'=4,'grp_0'=4,'grp_1'=2] {'dp_1'}, use_global_device_ids=true, to_apply=%region_30.31 | all-reduce | flops 1 | bytes 8 | tf_op jit(solution)/shard_map/psum | solution.py:39
  227.4 8.0 %psum.30 = f32[]{:T(128)} all-reduce(f32[]{:T(128)} %psum.29), channel_id=1, replica_groups=mesh['dp_0'=8,'dp_1'=4,'grp_0'=4,'grp_1'=2] {'grp_0'}, use_global_device_ids=true, to_apply=%region_31.32 | all-reduce | flops 1 | bytes 8 | tf_op jit(solution)/shard_map/psum | solution.py:39
  235.4 2.0 fusion.21
  237.4 2.0 fusion.15
  239.4 10.4 %psum.31 = f32[]{:T(128)} all-reduce(f32[]{:T(128)} %psum.30), channel_id=1, replica_groups=mesh['dp_0'=8,'dp_1'=4,'grp_0'=4,'grp_1'=2] {'grp_1'}, use_global_device_ids=true, to_apply=%region_32.33 | all-reduce | flops 1 | bytes 8 | tf_op jit(solution)/shard_map/psum | solution.py:39
  249.8 2.1 fusion.73
  251.9 0.7 fusion.76
  252.6 2.1 fusion.78
  254.8 0.7 fusion.81
  (54 shorter events, 0.6 us)
Async XLA Ops:
  7.2 5.5 %copy-start = (bf16[4,256,1024]{2,1,0:T(8,128)(2,1)S(1)}, bf16[4,256,1024]{2,1,0:T(8,128)(2,1)}, u32[]{:S(2)}) copy-start(bf16[4,256,1024]{2,1,0:T(8,128)(2,1)} %param.6) | copy-start | bytes 6291460
  7.2 7.8 %copy-start.14 = (s32[4]{0:T(128)S(1)}, s32[4]{0:T(128)}, u32[]{:S(2)}) copy-start(s32[4]{0:T(128)} %param.7) | copy-start | bytes 52
  7.2 124.3 %all-gather.4.cloned.1.call-start = ((), (), s32[]{:S(2)}) async-start(), calls=%async_computation | async-start | bytes 4210688 | tf_op jit(solution)/shard_map/all_gather | solution.py:23
  15.0 1.2 copy-start.6
  15.3 2.9 %copy-start.4 = (bf16[4,256,1024]{2,1,0:T(8,128)(2,1)S(1)}, bf16[4,256,1024]{2,1,0:T(8,128)(2,1)}, u32[]{:S(2)}) copy-start(bf16[4,256,1024]{2,1,0:T(8,128)(2,1)} %param.5) | copy-start | bytes 6291460
  16.3 1.9 copy-start.1
  104.4 4.4 %copy-start.2 = (f32[4,256,1024]{2,1,0:T(8,128)S(1)}, f32[4,256,1024]{2,1,0:T(8,128)}, u32[]{:S(2)}) copy-start(f32[4,256,1024]{2,1,0:T(8,128)} %copy-done.1) | copy-start | bytes 12582916
  104.4 4.6 %copy-start.7 = (f32[4,256,256]{1,2,0:T(8,128)S(1)}, f32[4,256,256]{1,2,0:T(8,128)}, u32[]{:S(2)}) copy-start(f32[4,256,256]{1,2,0:T(8,128)} %copy-done.6) | copy-start | bytes 3145732
  108.7 2.5 copy-start.9
  111.8 4.3 %copy-start.8 = (f32[4,256,256]{1,2,0:T(8,128)S(1)}, f32[4,256,256]{1,2,0:T(8,128)}, u32[]{:S(2)}) copy-start(f32[4,256,256]{1,2,0:T(8,128)} %copy-done.6) | copy-start | bytes 3145732
  111.8 4.3 %copy-start.11 = (bf16[4,256,256]{1,2,0:T(8,128)(2,1)S(1)}, bf16[4,256,256]{1,2,0:T(8,128)(2,1)}, u32[]{:S(2)}) copy-start(bf16[4,256,256]{1,2,0:T(8,128)(2,1)} %get-tuple-element.52) | copy-start | bytes 1572868
  111.8 5.3 %copy-start.3 = (f32[4,256,1024]{2,1,0:T(8,128)S(1)}, f32[4,256,1024]{2,1,0:T(8,128)}, u32[]{:S(2)}) copy-start(f32[4,256,1024]{2,1,0:T(8,128)} %copy-done.1) | copy-start | bytes 12582916
  111.8 5.5 %copy-start.10 = (bf16[4,256,1024]{2,1,0:T(8,128)(2,1)S(1)}, bf16[4,256,1024]{2,1,0:T(8,128)(2,1)}, u32[]{:S(2)}) copy-start(bf16[4,256,1024]{2,1,0:T(8,128)(2,1)} %copy-done.9) | copy-start | bytes 6291460
  117.3 1.6 copy-start.5
  140.8 109.0 %copy-start.12 = (bf16[4,1024]{1,0:T(4,128)(2,1)S(1)}, bf16[4,1024]{1,0:T(4,128)(2,1)}, u32[]{:S(2)}) copy-start(bf16[4,1024]{1,0:T(4,128)(2,1)} %param.8) | copy-start | bytes 24580
  143.1 109.5 %copy-start.13 = (bf16[4,1024]{1,0:T(4,128)(2,1)S(1)}, bf16[4,1024]{1,0:T(4,128)(2,1)}, u32[]{:S(2)}) copy-start(bf16[4,1024]{1,0:T(4,128)(2,1)} %param.9) | copy-start | bytes 24580
Sparse Core Ops, SparseCore 0:
  11.6 119.8 all-gather.3
where the time goes:
time: 266 us; the launch traced here: 264 us
  blocking collectives  100 us (38%)
  local copies, waits for them, and re-layouts  64.9 us (24%)
  other arithmetic  38.3 us (14%)
  matrix products  35.4 us (13%)
  between operations  17.4 us (7%)
  waiting for transfers between devices  7.87 us (3%)
    all_gather x1, blocking collectives, gather_turned(): lax.all_gather(both, axis, axis=0, tiled=True)  60.9 us
    psum x4, blocking collectives, over_axes(): array = lax.psum(array, axis)  39.1 us
    scatter-add x1, other arithmetic, pair_terms(): jnp.diagonal(logits)  26.1 us
    scatter-add x1, local copies, waits for them, and re-layouts, pair_terms(): jnp.diagonal(logits)  19.1 us
    select_n x1, local copies, waits for them, and re-layouts, pair_terms(): masked = jnp.where(both_valid, logits, MASK_FILL)  17.4 us
    mul x1, local copies, waits for them, and re-layouts, pair_terms(): FINE_SCALE * jnp.dot(group_unit.astype(jnp.bfloat16), token_unit.astype(j...  16.5 us
    dot_general x3, matrix products, pair_terms(): jnp.dot(group_unit.astype(jnp.bfloat16), token_unit.astype(jnp.bfloat16)....  10.6 us
    unnamed x33, local copies, waits for them, and re-layouts  9.52 us
  transfers between devices with their start and end apart: 1, of which 1 were waited for; matrix products, arithmetic and copies ran while one was open for 42% of the time, Pallas kernels for 0%

commit v1 on v0

v1 whole, which is shorter than its diff:
```python
import functools

import jax
import jax.numpy as jnp
from jax import lax
from jax.experimental import pallas as pl
from jax.experimental.pallas import tpu as pltpu
from jax.sharding import PartitionSpec as P

MESH = pl.DeviceIdType.MESH
F32 = jnp.float32
BF16 = jnp.bfloat16

RANGE_EPS = 1e-06
NORM_EPS = 1e-06
GLOBAL_SCALE = 100.0
FINE_SCALE = 50.0

NX, NY, NZ, NC = 4, 4, 8, 2
GROUP = 16
D = 1024
CH = D // 128
PAIRS = 4
ROWS = GROUP * PAIRS
SLOT = PAIRS * CH
T = 256
BLK = 64


def dot_nn(a, b):
    return lax.dot_general(a, b, (((1,), (0,)), ((), ())), preferred_element_type=F32)


def dot_nt(a, b):
    return lax.dot_general(a, b, (((1,), (1,)), ((), ())), preferred_element_type=F32)


def dot_tn(a, b):
    return lax.dot_general(a, b, (((0,), (0,)), ((), ())), preferred_element_type=F32)


def ring(d, n):
    return min(d, n - d)


A_OFFS = sorted(
    ((dx, dy) for dx in range(NX) for dy in range(NY) if (dx, dy) != (0, 0)),
    key=lambda o: -(ring(o[0], NX) + ring(o[1], NY)),
)
B_OFFS = sorted(
    ((dz, dc) for dz in range(NZ) for dc in range(NC) if (dz, dc) != (0, 0)),
    key=lambda o: -ring(o[0], NZ),
)


def fine_pair(pair, length, tok, pat, s_ref, q_ref, hi_ref, lo_ref, wb_ref, wq_ref, z_ref,
              e_ref, bp_ref, v_ref, x1_ref, d_ref, col_ref, ds_out, m_out, c_out):
    s_ref[...] = dot_nt(tok[...], pat[...])
    q_ref[...] = dot_nt(pat[...], pat[...]).astype(BF16)
    inv_len = 0.5 / jnp.full((1, 1), length, jnp.int32).astype(F32)

    for b in range(T // BLK):
        rows = pl.ds(b * BLK, BLK)
        s = s_ref[rows, :]
        low = jnp.min(s, 1, keepdims=True)
        high = jnp.max(s, 1, keepdims=True)
        inv = 1.0 / (high - low + RANGE_EPS)
        x = (s - low) * inv - 1.0 / T
        raw = jnp.maximum(x, 0.0)
        iw = 1.0 / jnp.sum(raw, 1, keepdims=True)
        wb_ref[rows, :] = (raw * iw).astype(BF16)
        tf = tok[rows, :].astype(F32)
        ti = lax.rsqrt(jnp.sum(tf * tf, 1, keepdims=True) + NORM_EPS)
        sp = s * ti
        hi = sp.astype(BF16)
        hi_ref[rows, :] = hi
        lo_ref[rows, :] = (sp - hi.astype(F32)).astype(BF16)
        col_ref[rows, 0:1] = low
        col_ref[rows, 1:2] = high
        col_ref[rows, 2:3] = inv
        col_ref[rows, 3:4] = iw
        col_ref[rows, 4:5] = ti

    wq_ref[...] = dot_nn(wb_ref[...], q_ref[...])
    z_ref[...] = dot_nt(wb_ref[...], hi_ref[...]) + dot_nt(wb_ref[...], lo_ref[...])

    lane = lax.broadcasted_iota(jnp.int32, (BLK, T), 1)
    lane_ok = lane < length
    col_sum = jnp.zeros((1, T), F32)
    loss = jnp.zeros((1, 1), F32)
    for b in range(T // BLK):
        rows = pl.ds(b * BLK, BLK)
        sub = b * BLK + lax.broadcasted_iota(jnp.int32, (BLK, 1), 0)
        row_ok = sub < length
        gg = jnp.maximum(jnp.sum(wb_ref[rows, :].astype(F32) * wq_ref[rows, :], 1, keepdims=True), 0.0)
        gi = lax.rsqrt(gg + NORM_EPS)
        z = z_ref[rows, :] * (FINE_SCALE * gi)
        e = jnp.where(jnp.logical_and(lane_ok, row_ok), jnp.exp(z), 0.0)
        z_ref[rows, :] = z
        e_ref[rows, :] = e
        rs = jnp.sum(e, 1, keepdims=True)
        col_sum = col_sum + jnp.sum(e, 0, keepdims=True)
        diag = jnp.sum(jnp.where(lane == sub, z, 0.0), 1, keepdims=True)
        per_row = jnp.where(row_ok, jnp.log(rs) - 2.0 * diag, 0.0)
        loss = loss + jnp.sum(per_row, 0, keepdims=True)
        col_ref[rows, 5:6] = gi
        col_ref[rows, 6:7] = jnp.where(row_ok, 1.0 / rs, 0.0)
    lane_row = lax.broadcasted_iota(jnp.int32, (1, T), 1) < length
    loss = loss + jnp.sum(jnp.where(lane_row, jnp.log(col_sum), 0.0), 1, keepdims=True)
    ic = jnp.where(lane_row, 1.0 / col_sum, 0.0)

    for b in range(T // BLK):
        rows = pl.ds(b * BLK, BLK)
        sub = b * BLK + lax.broadcasted_iota(jnp.int32, (BLK, 1), 0)
        row_ok = sub < length
        gi = col_ref[rows, 5:6]
        ir = col_ref[rows, 6:7]
        two = jnp.where(row_ok, 2.0, 0.0)
        g = e_ref[rows, :] * (ir + ic) - jnp.where(lane == sub, two, 0.0)
        r = jnp.sum(g * z_ref[rows, :], 1, keepdims=True) * inv_len
        bp_ref[rows, :] = (g * (gi * (FINE_SCALE * inv_len))).astype(BF16)
        coef = gi * gi * r
        v_ref[rows, :] = (wb_ref[rows, :].astype(F32) * (-coef)).astype(BF16)
        col_ref[rows, 7:8] = coef

    x1_ref[...] = dot_nn(bp_ref[...], hi_ref[...]) + dot_nn(bp_ref[...], lo_ref[...])
    d_ref[...] = dot_tn(bp_ref[...], wb_ref[...])
    m_out[pair] = dot_tn(v_ref[...], wb_ref[...]).astype(BF16)

    for b in range(T // BLK):
        rows = pl.ds(b * BLK, BLK)
        low = col_ref[rows, 0:1]
        high = col_ref[rows, 1:2]
        inv = col_ref[rows, 2:3]
        iw = col_ref[rows, 3:4]
        ti = col_ref[rows, 4:5]
        coef = col_ref[rows, 7:8]
        s = s_ref[rows, :]
        x = (s - low) * inv - 1.0 / T
        w = jnp.maximum(x, 0.0) * iw
        gate = jnp.where(x > 0.0, 1.0, jnp.where(x == 0.0, 0.5, 0.0))
        dw = x1_ref[rows, :] - coef * wq_ref[rows, :]
        mean = jnp.sum(dw * w, 1, keepdims=True)
        a = gate * (dw - mean) * (iw * inv)
        total = jnp.sum(a, 1, keepdims=True)
        at_high = jnp.where(s == high, 1.0, 0.0)
        at_low = jnp.where(s == low, 1.0, 0.0)
        to_high = total * (-1.0 / T) / jnp.sum(at_high, 1, keepdims=True)
        to_low = total * (1.0 / T - 1.0) / jnp.sum(at_low, 1, keepdims=True)
        d = d_ref[rows, :] * ti
        along = jnp.sum(d * s, 1, keepdims=True)
        ds = a + at_high * to_high + at_low * to_low + d
        ds_out[pair, rows, :] = ds.astype(BF16)
        c_out[pair, rows, :] = -(ti * ti) * along
    return loss * inv_len


def unit_rows(pooled):
    values = pooled.astype(F32)
    inverse = lax.rsqrt(jnp.sum(values * values, 1, keepdims=True) + NORM_EPS)
    return values * inverse, inverse


def exchange_kernel(len_ref, tok_hbm, pat_hbm, img_ref, txt_ref,
                    ds_out, m_out, c_out, gimg_out, gtxt_out, loss_out,
                    tok_v, pat_v, s_ref, q_ref, hi_ref, lo_ref, wb_ref, wq_ref, z_ref, e_ref,
                    bp_ref, v_ref, x1_ref, d_ref, col_ref,
                    stage, unit_a, unit_b, mat_a, mat_b, wide, half_a, half_b, part_a, part_b,
                    stat_a, stat_b, lse_a, lse_b, got_a, got_b, note_a, note_b, tell_a, tell_b,
                    fine_ref, in_sem, send_sem, recv_sem):
    dp = lax.axis_index("dp")
    grp = lax.axis_index("grp")
    z, y = dp // NY, dp % NY
    x, core = grp // NC, grp % NC
    u = y * NX + x
    v = z * NC + core

    def peer_a(off):
        px, py = (x + off[0]) % NX, (y + off[1]) % NY
        return (z * NY + py, px * NC + core), py * NX + px

    def peer_b(off):
        pz, pc = (z + off[0]) % NZ, (core + off[1]) % NC
        return (pz * NY + y, x * NC + pc), pz * NC + pc

    peers_a = [peer_a(o) for o in A_OFFS]
    peers_b = [peer_b(o) for o in B_OFFS]

    loads = []
    for n in range(PAIRS):
        loads.append((
            pltpu.make_async_copy(tok_hbm.at[n], tok_v.at[n], in_sem.at[0, n]),
            pltpu.make_async_copy(pat_hbm.at[n], pat_v.at[n], in_sem.at[1, n]),
        ))
        loads[-1][0].start()
        loads[-1][1].start()

    barrier = pltpu.get_barrier_semaphore()
    for (dev_a, _), (dev_b, _) in zip(peers_a, peers_b):
        pl.semaphore_signal(barrier, inc=1, device_id=dev_a, device_id_type=MESH)
        pl.semaphore_signal(barrier, inc=1, device_id=dev_b, device_id_type=MESH)

    def exchange(phase, src_a, dst_a, src_b, dst_b):
        copies = []
        for k in range(GROUP - 1):
            for side, peers, src, dst in ((0, peers_a, src_a, dst_a), (1, peers_b, src_b, dst_b)):
                dev, slot = peers[k]
                copies.append(pltpu.make_async_remote_copy(
                    src_ref=src(slot), dst_ref=dst,
                    send_sem=send_sem.at[phase, side, k], recv_sem=recv_sem.at[phase, side, k],
                    device_id=dev, device_id_type=MESH))
        for c in copies:
            c.start()
        return copies

    img_unit, img_inv = unit_rows(img_ref[...])
    txt_unit, txt_inv = unit_rows(txt_ref[...])
    img_half = img_unit.astype(BF16)
    txt_half = txt_unit.astype(BF16)
    matches = GLOBAL_SCALE * jnp.sum(
        jnp.sum(img_half.astype(F32) * txt_half.astype(F32), 1, keepdims=True), 0, keepdims=True)
    for half, dst in ((img_half, half_a), (txt_half, half_b)):
        wide_half = half.astype(F32)
        for c in range(CH):
            stage[pl.ds(c, PAIRS, stride=CH), :] = wide_half[:, c * 128:(c + 1) * 128]
        dst[...] = stage[...].astype(BF16)

    fine_refs = (s_ref, q_ref, hi_ref, lo_ref, wb_ref, wq_ref, z_ref, e_ref, bp_ref, v_ref,
                 x1_ref, d_ref, col_ref, ds_out, m_out, c_out)

    def run_pair(n):
        pltpu.make_async_copy(tok_hbm.at[n], tok_v.at[n], in_sem.at[0, n]).wait()
        pltpu.make_async_copy(pat_hbm.at[n], pat_v.at[n], in_sem.at[1, n]).wait()
        return fine_pair(n, len_ref[n], tok_v.at[n], pat_v.at[n], *fine_refs)

    fine_ref[...] = jnp.zeros_like(fine_ref)

    def step(n, carry):
        fine_ref[0:1, 0:1] += run_pair(n)
        return carry

    lax.fori_loop(0, 1, step, 0)
    pl.semaphore_wait(barrier, 2 * (GROUP - 1))

    own_a = pl.multiple_of(u * SLOT, SLOT)
    own_b = pl.multiple_of(v * SLOT, SLOT)
    first = exchange(
        0, lambda slot: half_a, unit_a.at[pl.ds(own_a, SLOT)],
        lambda slot: half_b, unit_b.at[pl.ds(own_b, SLOT)])
    unit_a[pl.ds(own_a, SLOT), :] = half_a[...]
    unit_b[pl.ds(own_b, SLOT), :] = half_b[...]

    lax.fori_loop(1, PAIRS, step, 0)
    for c in first:
        c.wait()

    for src, dst in ((unit_a, mat_a), (unit_b, mat_b)):
        wide[...] = src[...].astype(F32)
        for c in range(CH):
            dst[:, c * 128:(c + 1) * 128] = wide[pl.ds(c, ROWS, stride=CH), :].astype(BF16)

    logits = GLOBAL_SCALE * dot_nt(mat_a[...], mat_b[...])
    turned = GLOBAL_SCALE * dot_nt(mat_b[...], mat_a[...])
    scalar = fine_ref[0:1, 0:1] - matches
    for block, dst, row in ((turned, stat_a, u), (logits, stat_b, v)):
        top = jnp.max(block, 0, keepdims=True)
        dst[row, 0:1, 0:ROWS] = top
        dst[row, 1:2, 0:ROWS] = jnp.sum(jnp.exp(block - top), 0, keepdims=True)
        dst[row, 2:3, :] = jnp.broadcast_to(scalar, (1, 128))
    second = exchange(
        1, lambda slot: stat_a.at[u], stat_a.at[u], lambda slot: stat_b.at[v], stat_b.at[v])
    for c in second:
        c.wait()

    def combine(stat):
        top = stat[0, 0:1, 0:ROWS]
        for k in range(1, GROUP):
            top = jnp.maximum(top, stat[k, 0:1, 0:ROWS])
        total = jnp.zeros((1, ROWS), F32)
        for k in range(GROUP):
            total = total + stat[k, 1:2, 0:ROWS] * jnp.exp(stat[k, 0:1, 0:ROWS] - top)
        return top + jnp.log(total)

    row_lse = combine(stat_a)
    col_lse = combine(stat_b)
    fine_sum = stat_a[0, 2:3, 0:1]
    for k in range(1, GROUP):
        fine_sum = fine_sum + stat_a[k, 2:3, 0:1]
    tell_b[...] = jnp.broadcast_to(
        fine_sum + 0.5 * jnp.sum(row_lse, 1, keepdims=True), tell_b.shape)
    tell_a[...] = jnp.broadcast_to(0.5 * jnp.sum(col_lse, 1, keepdims=True), tell_a.shape)

    i_at = lax.broadcasted_iota(jnp.int32, (ROWS, ROWS), 0)
    j_at = lax.broadcasted_iota(jnp.int32, (ROWS, ROWS), 1)

    def same(img_at, txt_at):
        off = img_at - PAIRS * u
        inside = jnp.logical_and(off >= 0, off < PAIRS)
        return jnp.where(jnp.logical_and(inside, off == txt_at - PAIRS * v), 0.5, 0.0)

    row_part = (0.5 * jnp.exp(turned - row_lse) - same(j_at, i_at)).astype(BF16)
    col_part = (0.5 * jnp.exp(logits - col_lse) - same(i_at, j_at)).astype(BF16)
    for c in range(CH):
        cols = slice(c * 128, (c + 1) * 128)
        txt_c = mat_b[:, cols]
        img_c = mat_a[:, cols]
        part_a[pl.ds(c, ROWS, stride=CH), :] = dot_tn(row_part, txt_c) + dot_nn(col_part, txt_c)
        part_b[pl.ds(c, ROWS, stride=CH), :] = dot_nn(row_part, img_c) + dot_tn(col_part, img_c)

    def piece(ref):
        return lambda slot: ref.at[pl.ds(pl.multiple_of(slot * SLOT, SLOT), SLOT)]

    third = exchange(
        2, piece(part_a), got_a.at[pl.ds(own_a, SLOT)], piece(part_b), got_b.at[pl.ds(own_b, SLOT)])
    notes = exchange(3, lambda slot: tell_a, note_a.at[u], lambda slot: tell_b, note_b.at[v])
    got_a[pl.ds(own_a, SLOT), :] = part_a[pl.ds(own_a, SLOT), :]
    got_b[pl.ds(own_b, SLOT), :] = part_b[pl.ds(own_b, SLOT), :]
    note_a[u] = tell_a[...]
    note_b[v] = tell_b[...]
    for c in third:
        c.wait()
    for c in notes:
        c.wait()

    for got, unit, inv, out in ((got_a, img_unit, img_inv, gimg_out), (got_b, txt_unit, txt_inv, gtxt_out)):
        total = got[0:SLOT, :]
        for k in range(1, GROUP):
            total = total + got[k * SLOT:(k + 1) * SLOT, :]
        stage[...] = GLOBAL_SCALE * total
        along = jnp.zeros((PAIRS, 1), F32)
        for c in range(CH):
            along = along + jnp.sum(
                stage[pl.ds(c, PAIRS, stride=CH), :] * unit[:, c * 128:(c + 1) * 128], 1, keepdims=True)
        for c in range(CH):
            cols = slice(c * 128, (c + 1) * 128)
            part = stage[pl.ds(c, PAIRS, stride=CH), :]
            out[:, cols] = ((part - unit[:, cols] * along) * inv).astype(BF16)
    total = note_a[0, 0:1, 0:1] + note_b[0, 0:1, 0:1]
    for k in range(1, GROUP):
        total = total + note_a[k, 0:1, 0:1] + note_b[k, 0:1, 0:1]
    loss_out[...] = total * (1.0 / (GROUP * GROUP * PAIRS))


def apply_kernel(tok_ref, pat_ref, ds_ref, m_ref, c_ref, gimg_ref, gtxt_ref, loss_ref,
                 gtok_out, gpat_out, gimg_out, gtxt_out, loss_out):
    ds = ds_ref[0]
    m = m_ref[0]
    c = c_ref[0]
    for k in range(D // 256):
        cols = slice(k * 256, (k + 1) * 256)
        tok = tok_ref[0, :, cols]
        pat = pat_ref[0, :, cols]
        gtok_out[0, :, cols] = (dot_nn(ds, pat) + c * tok.astype(F32)).astype(BF16)
        gpat_out[0, :, cols] = (dot_tn(ds, tok) + dot_nn(m, pat)).astype(BF16)
    gimg_out[...] = gimg_ref[...]
    gtxt_out[...] = gtxt_ref[...]
    loss_out[...] = loss_ref[...]


def body(tokens, patches, lengths, img_pooled, txt_pooled):
    vmem = pl.BlockSpec(memory_space=pltpu.VMEM)
    smem = pl.BlockSpec(memory_space=pltpu.SMEM)
    hbm = pl.BlockSpec(memory_space=pl.ANY)
    sds = jax.ShapeDtypeStruct
    vm = pltpu.VMEM
    ds, m, c, gimg, gtxt, loss = pl.pallas_call(
        exchange_kernel,
        name="exchange",
        out_shape=(
            sds((PAIRS, T, T), BF16), sds((PAIRS, T, T), BF16), sds((PAIRS, T, 1), F32),
            sds((PAIRS, D), BF16), sds((PAIRS, D), BF16), sds((1, 1), F32)),
        in_specs=[smem, hbm, hbm, vmem, vmem],
        out_specs=(vmem,) * 6,
        scratch_shapes=[
            vm((PAIRS, T, D), BF16), vm((PAIRS, T, D), BF16),
            vm((T, T), F32), vm((T, T), BF16), vm((T, T), BF16), vm((T, T), BF16), vm((T, T), BF16),
            vm((T, T), F32), vm((T, T), F32), vm((T, T), F32), vm((T, T), BF16), vm((T, T), BF16),
            vm((T, T), F32), vm((T, T), F32), vm((T, 128), F32),
            vm((SLOT, 128), F32), vm((GROUP * SLOT, 128), BF16), vm((GROUP * SLOT, 128), BF16),
            vm((ROWS, D), BF16), vm((ROWS, D), BF16), vm((GROUP * SLOT, 128), F32),
            vm((SLOT, 128), BF16), vm((SLOT, 128), BF16),
            vm((GROUP * SLOT, 128), F32), vm((GROUP * SLOT, 128), F32),
            vm((GROUP, 4, 128), F32), vm((GROUP, 4, 128), F32), vm((1, ROWS), F32), vm((1, ROWS), F32),
            vm((GROUP * SLOT, 128), F32), vm((GROUP * SLOT, 128), F32),
            vm((GROUP, 1, 128), F32), vm((GROUP, 1, 128), F32), vm((1, 128), F32), vm((1, 128), F32),
            vm((8, 128), F32),
            pltpu.SemaphoreType.DMA((2, PAIRS)),
            pltpu.SemaphoreType.DMA((4, 2, GROUP - 1)),
            pltpu.SemaphoreType.DMA((4, 2, GROUP - 1)),
        ],
        compiler_params=pltpu.CompilerParams(
            collective_id=0, has_side_effects=True, vmem_limit_bytes=56 << 20),
    )(lengths, tokens, patches, img_pooled, txt_pooled)

    def block(*shape):
        return pl.BlockSpec((1,) + shape, lambda n: (n,) + (0,) * len(shape))

    def fixed(*shape):
        return pl.BlockSpec(shape, lambda n: (0,) * len(shape))

    gtok, gpat, gimg, gtxt, loss = pl.pallas_call(
        apply_kernel,
        name="apply",
        grid=(PAIRS,),
        out_shape=(
            sds((PAIRS, T, D), BF16), sds((PAIRS, T, D), BF16),
            sds((PAIRS, D), BF16), sds((PAIRS, D), BF16), sds((1, 1), F32)),
        in_specs=[block(T, D), block(T, D), block(T, T), block(T, T), block(T, 1),
                  fixed(PAIRS, D), fixed(PAIRS, D), fixed(1, 1)],
        out_specs=(block(T, D), block(T, D), fixed(PAIRS, D), fixed(PAIRS, D), fixed(1, 1)),
        compiler_params=pltpu.CompilerParams(
            dimension_semantics=("arbitrary",), vmem_limit_bytes=32 << 20),
    )(tokens, patches, ds, m, c, gimg, gtxt, loss)
    return gtok, gpat, gimg, gtxt, loss.reshape(())


def solution(mesh):
    both = ("dp", "grp")
    placed = (P(both, None, None), P(both, None, None), P(both), P(both, None), P(both, None))
    return jax.shard_map(
        body,
        mesh=mesh,
        in_specs=placed,
        out_specs=(P(both, None, None), P(both, None, None), P(both, None), P(both, None), P()),
        check_vma=False,
    )
```

time: 266 us -> 48.6 us (0.18)
  blocking collectives: 100 us -> 0 us
  local copies, waits for them, and re-layouts: 64.9 us -> 4.52 us
  Pallas kernels: 0 us -> 43.1 us
  other arithmetic: 38.3 us -> 0 us
  matrix products: 35.4 us -> 0 us
  between operations: 17.4 us -> 0.68 us
  waiting for transfers between devices: 7.87 us -> 0 us
    all_gather x1 -> x0, blocking collectives: 60.9 us -> none  [gather_turned(): lax.all_gather(both, axis, axis=0, tiled=True)]
    pallas_call x0 -> x2, Pallas kernels: none -> 43.1 us  [the longest x1 39.1 us: body(): pl.pallas_call(exchange_kernel, name='exchange', out_shape=(sds((PAIRS, T...]
    psum x4 -> x0, blocking collectives: 39.1 us -> none  [over_axes(): array = lax.psum(array, axis)]
    dot_general x15 -> x0, matrix products: 35.4 us -> none  [the longest x3 10.6 us: pair_terms(): jnp.dot(group_unit.astype(jnp.bfloat16), token_unit.astype(jnp.bfloat16)....]
    scatter-add x1 -> x0, other arithmetic: 26.1 us -> none  [pair_terms(): jnp.diagonal(logits)]
    scatter-add x1 -> x0, local copies, waits for them, and re-layouts: 19.1 us -> none  [pair_terms(): jnp.diagonal(logits)]
    select_n x1 -> x0, local copies, waits for them, and re-layouts: 17.4 us -> none  [pair_terms(): masked = jnp.where(both_valid, logits, MASK_FILL)]
    mul x2 -> x0, local copies, waits for them, and re-layouts: 16.6 us -> none  [the longest x1 16.5 us: pair_terms(): FINE_SCALE * jnp.dot(group_unit.astype(jnp.bfloat16), token_unit.astype(j...]
  transfers between devices with their start and end apart: 1 -> 0, of which waited for: 1 -> 0; matrix products, arithmetic and copies ran while one was open for 42% -> 0% of each run, Pallas kernels for 0% -> 0%
where the time goes in v1:
time: 48.6 us; the launch traced here: 48.3 us
  Pallas kernels  43.1 us (89%)
  local copies, waits for them, and re-layouts  4.52 us (9%)
  between operations  0.68 us (1%)
    pallas_call x1, Pallas kernels, body(): pl.pallas_call(exchange_kernel, name='exchange', out_shape=(sds((PAIRS, T...  39.1 us
    unnamed x14, local copies, waits for them, and re-layouts  4.52 us
    pallas_call x1, Pallas kernels, body(): pl.pallas_call(apply_kernel, name='apply', grid=(PAIRS,), out_shape=(sds(...  4.02 us

profile of v1, /device:TPU:1, one launch (start us, length us, event | category | flops | bytes accessed | tf_op | source)
XLA Modules:
  0.0 48.3 jit_solution(6745682284312790104)
XLA Ops:
  0.6 0.0 copy-start.1
  0.6 0.0 copy-start
  0.7 39.1 %exchange.1 = (bf16[4,256,256]{2,1,0:T(8,128)(2,1)}, bf16[4,256,256]{2,1,0:T(8,128)(2,1)}, f32[4,256,1]{2,1,0:T(8,128)}, bf16[4,1024]{1,0:T(4,128)(2,1)}, bf16[4,1024]{1,0:T(4,128)(2,1)}, /*index=5*/f32[1,1]{1,0:T(1,128)}) custom-call(s32[4]{0:T(128)} %len_ref.1, bf16[4,256,1024]{2,1,0:T(8,128)(2,1)} %tok_ref.1, bf16[4,256,1024]{2,1,0:T(8,128)(2,1)} %pat_ref.1, ...), custom_call_target="tpu_custom_call" | custom-call | tf_op jit(solution)/shard_map/exchange/pallas_call | solution.py:366
  39.7 0.0 copy-done.1
  39.7 0.0 copy-done
  39.7 0.0 copy-start.2
  39.7 1.0 %copy-done.2 = bf16[4,256,256]{2,1,0:T(8,128)(2,1)S(1)} copy-done((bf16[4,256,256]{2,1,0:T(8,128)(2,1)S(1)}, bf16[4,256,256]{2,1,0:T(8,128)(2,1)}, u32[]{:S(2)}) %copy-start.2) | copy-done | bytes 524312
  40.8 0.0 copy-start.3
  40.8 1.0 %copy-done.3 = bf16[4,256,256]{2,1,0:T(8,128)(2,1)S(1)} copy-done((bf16[4,256,256]{2,1,0:T(8,128)(2,1)S(1)}, bf16[4,256,256]{2,1,0:T(8,128)(2,1)}, u32[]{:S(2)}) %copy-start.3) | copy-done | bytes 524312
  41.8 0.0 copy-start.4
  41.8 1.0 %copy-done.4 = f32[4,256,1]{2,1,0:T(8,128)S(1)} copy-done((f32[4,256,1]{2,1,0:T(8,128)S(1)}, f32[4,256,1]{2,1,0:T(8,128)}, u32[]{:S(2)}) %copy-start.4) | copy-done | bytes 4120
  42.9 0.0 copy-start.5
  42.9 0.7 %copy-done.5 = bf16[4,1024]{1,0:T(4,128)(2,1)S(1)} copy-done((bf16[4,1024]{1,0:T(4,128)(2,1)S(1)}, bf16[4,1024]{1,0:T(4,128)(2,1)}, u32[]{:S(2)}) %copy-start.5) | copy-done | bytes 8216
  43.6 0.0 copy-start.6
  43.6 0.7 %copy-done.6 = bf16[4,1024]{1,0:T(4,128)(2,1)S(1)} copy-done((bf16[4,1024]{1,0:T(4,128)(2,1)S(1)}, bf16[4,1024]{1,0:T(4,128)(2,1)}, u32[]{:S(2)}) %copy-start.6) | copy-done | bytes 8216
  44.3 4.0 %apply.1 = (bf16[4,256,1024]{2,1,0:T(8,128)(2,1)}, bf16[4,256,1024]{2,1,0:T(8,128)(2,1)}, bf16[4,1024]{1,0:T(4,128)(2,1)}, bf16[4,1024]{1,0:T(4,128)(2,1)}, f32[1,1]{1,0:T(1,128)}) custom-call(bf16[4,256,1024]{2,1,0:T(8,128)(2,1)S(1)} %copy-done, bf16[4,256,1024]{2,1,0:T(8,128)(2,1)S(1)} %copy-done.1, bf16[4,256,256]{2,1,0:T(8,128)(2,1)S(1)} %copy-done.2, ...), custom_call_target="tpu_custom_call" | custom-call | tf_op jit(solution)/shard_map/apply/pallas_call | solution.py:401
Async XLA Ops:
  0.6 39.1 %copy-start.1 = (bf16[4,256,1024]{2,1,0:T(8,128)(2,1)S(1)}, bf16[4,256,1024]{2,1,0:T(8,128)(2,1)}, u32[]{:S(2)}) copy-start(bf16[4,256,1024]{2,1,0:T(8,128)(2,1)} %pat_ref.1) | copy-start | bytes 6291460
  0.6 39.1 %copy-start = (bf16[4,256,1024]{2,1,0:T(8,128)(2,1)S(1)}, bf16[4,256,1024]{2,1,0:T(8,128)(2,1)}, u32[]{:S(2)}) copy-start(bf16[4,256,1024]{2,1,0:T(8,128)(2,1)} %tok_ref.1) | copy-start | bytes 6291460
  39.7 1.0 %copy-start.2 = (bf16[4,256,256]{2,1,0:T(8,128)(2,1)S(1)}, bf16[4,256,256]{2,1,0:T(8,128)(2,1)}, u32[]{:S(2)}) copy-start(bf16[4,256,256]{2,1,0:T(8,128)(2,1)} %get-tuple-element.16.ds_ref) | copy-start | bytes 1572868
  40.8 1.0 %copy-start.3 = (bf16[4,256,256]{2,1,0:T(8,128)(2,1)S(1)}, bf16[4,256,256]{2,1,0:T(8,128)(2,1)}, u32[]{:S(2)}) copy-start(bf16[4,256,256]{2,1,0:T(8,128)(2,1)} %get-tuple-element.17.m_ref) | copy-start | bytes 1572868
  41.8 1.0 %copy-start.4 = (f32[4,256,1]{2,1,0:T(8,128)S(1)}, f32[4,256,1]{2,1,0:T(8,128)}, u32[]{:S(2)}) copy-start(f32[4,256,1]{2,1,0:T(8,128)} %get-tuple-element.18.c_ref) | copy-start | bytes 12292
  42.9 0.7 %copy-start.5 = (bf16[4,1024]{1,0:T(4,128)(2,1)S(1)}, bf16[4,1024]{1,0:T(4,128)(2,1)}, u32[]{:S(2)}) copy-start(bf16[4,1024]{1,0:T(4,128)(2,1)} %get-tuple-element.19.gimg_ref) | copy-start | bytes 24580
  43.6 0.7 %copy-start.6 = (bf16[4,1024]{1,0:T(4,128)(2,1)S(1)}, bf16[4,1024]{1,0:T(4,128)(2,1)}, u32[]{:S(2)}) copy-start(bf16[4,1024]{1,0:T(4,128)(2,1)} %get-tuple-element.20.gtxt_ref) | copy-start | bytes 24580

commit v2 on v1

v2 whole, which is shorter than its diff:
```python
import functools

import jax
import jax.numpy as jnp
from jax import lax
from jax.experimental import pallas as pl
from jax.experimental.pallas import tpu as pltpu
from jax.sharding import PartitionSpec as P

MESH = pl.DeviceIdType.MESH
F32 = jnp.float32
BF16 = jnp.bfloat16

RANGE_EPS = 1e-06
NORM_EPS = 1e-06
GLOBAL_SCALE = 100.0
FINE_SCALE = 50.0

NX, NY, NZ, NC = 4, 4, 8, 2
GROUP = 16
D = 1024
CH = D // 128
PAIRS = 4
ROWS = GROUP * PAIRS
SLOT = PAIRS * CH
T = 256
LOG2_E = 1.4426950408889634


def dot_nn(a, b):
    return lax.dot_general(a, b, (((1,), (0,)), ((), ())), preferred_element_type=F32)


def dot_nt(a, b):
    return lax.dot_general(a, b, (((1,), (1,)), ((), ())), preferred_element_type=F32)


def dot_tn(a, b):
    return lax.dot_general(a, b, (((0,), (0,)), ((), ())), preferred_element_type=F32)


def ring(d, n):
    return min(d, n - d)


A_OFFS = sorted(
    ((dx, dy) for dx in range(NX) for dy in range(NY) if (dx, dy) != (0, 0)),
    key=lambda o: -(ring(o[0], NX) + ring(o[1], NY)),
)
B_OFFS = sorted(
    ((dz, dc) for dz in range(NZ) for dc in range(NC) if (dz, dc) != (0, 0)),
    key=lambda o: -ring(o[0], NZ),
)


def fine_losses(pair, length, tok, pat, st, hi, lo, wb, wq, zt, et, bp, m, rowv, colv):
    st[pair] = dot_nt(pat[...], tok[...])
    q = dot_nt(pat[...], pat[...]).astype(BF16)
    squares = tok[...] * tok[...]
    norm = dot_nn(squares, jnp.ones((D, 128), BF16))
    ti = lax.rsqrt(norm + NORM_EPS)
    inv_len = 0.5 / jnp.full((1, 1), length, jnp.int32).astype(F32)

    for h in range(2):
        cols = slice(h * 128, (h + 1) * 128)
        s = st[pair, :, cols]
        low = jnp.min(s, 0, keepdims=True)
        high = jnp.max(s, 0, keepdims=True)
        inv = 1.0 / (high - low + RANGE_EPS)
        raw = jnp.maximum((s - low) * inv - 1.0 / T, 0.0)
        iw = 1.0 / jnp.sum(raw, 0, keepdims=True)
        wb[pair, :, cols] = (raw * iw).astype(BF16)
        top = s.astype(BF16)
        hi[pair, :, cols] = top
        lo[pair, :, cols] = (s - top.astype(F32)).astype(BF16)
        rowv[pair, 0:1, cols] = low
        rowv[pair, 1:2, cols] = high
        rowv[pair, 2:3, cols] = inv
        rowv[pair, 3:4, cols] = iw

    wq[pair] = dot_nn(q, wb[pair])
    zt[...] = dot_tn(hi[pair], wb[pair]) + dot_tn(lo[pair], wb[pair])

    k_at = lax.broadcasted_iota(jnp.int32, (T, 1), 0)
    t_at = lax.broadcasted_iota(jnp.int32, (1, T), 1)
    scale_k = ti * (FINE_SCALE * LOG2_E)
    over_t = jnp.zeros((T, 128), F32)
    loss = jnp.zeros((1, 1), F32)
    for h in range(2):
        cols = slice(h * 128, (h + 1) * 128)
        ok = t_at[:, cols] < length
        gg = jnp.sum(wb[pair, :, cols].astype(F32) * wq[pair, :, cols], 0, keepdims=True)
        gi = lax.rsqrt(jnp.maximum(gg, 0.0) + NORM_EPS)
        z = zt[:, cols] * scale_k * gi
        e = jnp.where(jnp.logical_and(k_at < length, ok), jnp.exp2(z), 0.0)
        zt[:, cols] = z
        et[:, cols] = e
        rs = jnp.sum(e, 0, keepdims=True)
        over_t = over_t + e
        rowv[pair, 4:5, cols] = gi
        rowv[pair, 5:6, cols] = jnp.where(ok, 1.0 / rs, 0.0)
        loss = loss + jnp.sum(jnp.where(ok, jnp.log(rs), 0.0), 1, keepdims=True)
    cs = jnp.sum(over_t, 1, keepdims=True)
    k_ok = k_at < length
    loss = loss + jnp.sum(jnp.where(k_ok, jnp.log(cs), 0.0), 0, keepdims=True)
    ic = jnp.where(k_ok, 1.0 / cs, 0.0)

    bp_k = ti * (FINE_SCALE * inv_len)
    over_t = [jnp.zeros((128, 128), F32)] * 2
    for h in range(2):
        cols = slice(h * 128, (h + 1) * 128)
        gi = rowv[pair, 4:5, cols]
        ir = rowv[pair, 5:6, cols]
        r = jnp.zeros((1, 128), F32)
        for b in range(2):
            rows = slice(b * 128, (b + 1) * 128)
            z = zt[rows, cols]
            g = et[rows, cols] * (ir + ic[rows, :])
            if b == h:
                own = k_at[rows, :] == t_at[:, cols]
                both = jnp.logical_and(own, t_at[:, cols] < length)
                g = g - jnp.where(both, 2.0, 0.0)
                diag = jnp.sum(jnp.where(both, z, 0.0), 0, keepdims=True)
                loss = loss - (2.0 / LOG2_E) * jnp.sum(diag, 1, keepdims=True)
            prod = g * z
            r = r + jnp.sum(prod, 0, keepdims=True)
            over_t[b] = over_t[b] + prod
            bp[pair, rows, cols] = (g * gi * bp_k[rows, :]).astype(BF16)
        coef = gi * gi * r * (inv_len / LOG2_E)
        rowv[pair, 6:7, cols] = coef
        et[:, cols] = wb[pair, :, cols].astype(F32) * (-coef)
    for b in range(2):
        rows = slice(b * 128, (b + 1) * 128)
        along = jnp.sum(over_t[b], 1, keepdims=True) * (inv_len / LOG2_E)
        colv[pair, rows, :] = (-along * ti[rows, :] * ti[rows, :]).astype(BF16)
    m[pair] = dot_nt(et[...].astype(BF16), wb[pair]).astype(BF16)
    return loss * inv_len


def fine_grads(pair, tok, pat, st, hi, lo, wb, wq, x1, d, bp, ds, m, rowv, colv, gtok, gpat):
    x1[...] = dot_nn(hi[pair], bp[pair]) + dot_nn(lo[pair], bp[pair])
    d[...] = dot_nt(wb[pair], bp[pair])
    for h in range(2):
        cols = slice(h * 128, (h + 1) * 128)
        low = rowv[pair, 0:1, cols]
        high = rowv[pair, 1:2, cols]
        inv = rowv[pair, 2:3, cols]
        iw = rowv[pair, 3:4, cols]
        coef = rowv[pair, 6:7, cols]
        s = st[pair, :, cols]
        x = (s - low) * inv - 1.0 / T
        w = jnp.maximum(x, 0.0) * iw
        dw = x1[:, cols] - coef * wq[pair, :, cols]
        mean = jnp.sum(dw * w, 0, keepdims=True)
        slope = iw * inv
        gate = jnp.where(x > 0.0, slope, jnp.where(x == 0.0, 0.5 * slope, 0.0))
        a = gate * (dw - mean)
        total = jnp.sum(a, 0, keepdims=True)
        at_high = s == high
        at_low = s == low
        n_high = jnp.sum(jnp.where(at_high, 1.0, 0.0), 0, keepdims=True)
        n_low = jnp.sum(jnp.where(at_low, 1.0, 0.0), 0, keepdims=True)
        to_high = total * (-1.0 / T) / n_high
        to_low = total * (1.0 / T - 1.0) / n_low
        ends = jnp.where(at_high, to_high, jnp.where(at_low, to_low, 0.0))
        ds[:, cols] = (a + ends + d[:, cols]).astype(BF16)
    c = jnp.concatenate([colv[pair], colv[pair]], 1)
    for k in range(D // 256):
        cols = slice(k * 256, (k + 1) * 256)
        gtok[pair, :, cols] = dot_tn(ds[...], pat[:, cols]).astype(BF16) + c * tok[:, cols]
        gpat[pair, :, cols] = (dot_nn(ds[...], tok[:, cols]) + dot_nn(m[pair], pat[:, cols])).astype(BF16)


def unit_rows(pooled):
    values = pooled.astype(F32)
    inverse = lax.rsqrt(jnp.sum(values * values, 1, keepdims=True) + NORM_EPS)
    return values * inverse, inverse


def exchange_kernel(len_hbm, tok_hbm, pat_hbm, img_hbm, txt_hbm,
                    gtok_out, gpat_out, gimg_out, gtxt_out, loss_out,
                    tok_v, pat_v, st, hi, lo, wb, wq, zt, et, bp, ds, m, rowv, colv,
                    stage, unit_a, unit_b, mat_a, mat_b, wide, half_a, half_b, part_a, part_b,
                    whole_a, whole_b, stat_a, stat_b, got_a, got_b, note_a, note_b, tell_a, tell_b,
                    fine_ref, len_ref, img_ref, txt_ref, in_sem, small_sem, send_sem, recv_sem):
    dp = lax.axis_index("dp")
    grp = lax.axis_index("grp")
    z, y = dp // NY, dp % NY
    x, core = grp // NC, grp % NC
    u = y * NX + x
    v = z * NC + core

    def peer_a(off):
        px, py = (x + off[0]) % NX, (y + off[1]) % NY
        return (z * NY + py, px * NC + core), py * NX + px

    def peer_b(off):
        pz, pc = (z + off[0]) % NZ, (core + off[1]) % NC
        return (pz * NY + y, x * NC + pc), pz * NC + pc

    peers_a = [peer_a(o) for o in A_OFFS]
    peers_b = [peer_b(o) for o in B_OFFS]

    small = [pltpu.make_async_copy(src, dst, small_sem.at[k]) for k, (src, dst) in enumerate(
        ((len_hbm, len_ref), (img_hbm, img_ref), (txt_hbm, txt_ref)))]
    for c in small:
        c.start()
    loads = []
    for n in range(PAIRS):
        loads.append((
            pltpu.make_async_copy(tok_hbm.at[n], tok_v.at[n], in_sem.at[0, n]),
            pltpu.make_async_copy(pat_hbm.at[n], pat_v.at[n], in_sem.at[1, n]),
        ))
        loads[-1][0].start()
        loads[-1][1].start()

    barrier = pltpu.get_barrier_semaphore()
    for (dev_a, _), (dev_b, _) in zip(peers_a, peers_b):
        pl.semaphore_signal(barrier, inc=1, device_id=dev_a, device_id_type=MESH)
        pl.semaphore_signal(barrier, inc=1, device_id=dev_b, device_id_type=MESH)

    def exchange(phase, src_a, dst_a, src_b, dst_b):
        copies = []
        for k in range(GROUP - 1):
            for side, peers, src, dst in ((0, peers_a, src_a, dst_a), (1, peers_b, src_b, dst_b)):
                dev, slot = peers[k]
                copies.append(pltpu.make_async_remote_copy(
                    src_ref=src(slot), dst_ref=dst,
                    send_sem=send_sem.at[phase, side, k], recv_sem=recv_sem.at[phase, side, k],
                    device_id=dev, device_id_type=MESH))
        for c in copies:
            c.start()
        return copies

    for c in small:
        c.wait()
    img_unit, img_inv = unit_rows(img_ref[...])
    txt_unit, txt_inv = unit_rows(txt_ref[...])
    img_half = img_unit.astype(BF16)
    txt_half = txt_unit.astype(BF16)
    matches = GLOBAL_SCALE * jnp.sum(
        jnp.sum(img_half.astype(F32) * txt_half.astype(F32), 1, keepdims=True), 0, keepdims=True)
    for half, dst in ((img_half, half_a), (txt_half, half_b)):
        wide_half = half.astype(F32)
        for c in range(CH):
            stage[pl.ds(c, PAIRS, stride=CH), :] = wide_half[:, c * 128:(c + 1) * 128]
        dst[...] = stage[...].astype(BF16)

    def losses(n, carry):
        pltpu.make_async_copy(tok_hbm.at[n], tok_v.at[n], in_sem.at[0, n]).wait()
        pltpu.make_async_copy(pat_hbm.at[n], pat_v.at[n], in_sem.at[1, n]).wait()
        fine_ref[0:1, 0:1] += fine_losses(
            n, len_ref[n], tok_v.at[n], pat_v.at[n], st, hi, lo, wb, wq, zt, et, bp, m, rowv, colv)
        return carry

    def grads(n, carry):
        fine_grads(n, tok_v.at[n], pat_v.at[n], st, hi, lo, wb, wq, zt, et, bp, ds, m, rowv, colv,
                   gtok_out, gpat_out)
        return carry

    fine_ref[...] = jnp.zeros_like(fine_ref)
    lax.fori_loop(0, 1, losses, 0)
    pl.semaphore_wait(barrier, 2 * (GROUP - 1))

    own_a = pl.multiple_of(u * SLOT, SLOT)
    own_b = pl.multiple_of(v * SLOT, SLOT)
    first = exchange(
        0, lambda slot: half_a, unit_a.at[pl.ds(own_a, SLOT)],
        lambda slot: half_b, unit_b.at[pl.ds(own_b, SLOT)])
    unit_a[pl.ds(own_a, SLOT), :] = half_a[...]
    unit_b[pl.ds(own_b, SLOT), :] = half_b[...]

    lax.fori_loop(1, PAIRS, losses, 0)
    for c in first:
        c.wait()

    for src, dst in ((unit_a, mat_a), (unit_b, mat_b)):
        wide[...] = src[...].astype(F32)
        for c in range(CH):
            dst[:, c * 128:(c + 1) * 128] = wide[pl.ds(c, ROWS, stride=CH), :].astype(BF16)

    logits = GLOBAL_SCALE * dot_nt(mat_a[...], mat_b[...])
    turned = GLOBAL_SCALE * dot_nt(mat_b[...], mat_a[...])
    scalar = fine_ref[0:1, 0:1] - matches
    for block, dst, row in ((turned, stat_a, u), (logits, stat_b, v)):
        top = jnp.max(block, 0, keepdims=True)
        dst[row, 0:1, 0:ROWS] = top
        dst[row, 1:2, 0:ROWS] = jnp.sum(jnp.exp(block - top), 0, keepdims=True)
        dst[row, 2:3, :] = jnp.broadcast_to(scalar, (1, 128))
    second = exchange(
        1, lambda slot: stat_a.at[u], stat_a.at[u], lambda slot: stat_b.at[v], stat_b.at[v])
    lax.fori_loop(0, 2, grads, 0)
    for c in second:
        c.wait()

    def combine(stat):
        top = stat[0, 0:1, 0:ROWS]
        for k in range(1, GROUP):
            top = jnp.maximum(top, stat[k, 0:1, 0:ROWS])
        total = jnp.zeros((1, ROWS), F32)
        for k in range(GROUP):
            total = total + stat[k, 1:2, 0:ROWS] * jnp.exp(stat[k, 0:1, 0:ROWS] - top)
        return top + jnp.log(total)

    row_lse = combine(stat_a)
    col_lse = combine(stat_b)
    fine_sum = stat_a[0, 2:3, 0:1]
    for k in range(1, GROUP):
        fine_sum = fine_sum + stat_a[k, 2:3, 0:1]
    lane_at = lax.broadcasted_iota(jnp.int32, (1, 128), 1)
    say_b = fine_sum + 0.5 * jnp.sum(row_lse, 1, keepdims=True)
    say_a = 0.5 * jnp.sum(col_lse, 1, keepdims=True)

    i_at = lax.broadcasted_iota(jnp.int32, (ROWS, ROWS), 0)
    j_at = lax.broadcasted_iota(jnp.int32, (ROWS, ROWS), 1)

    def same(img_at, txt_at):
        off = img_at - PAIRS * u
        inside = jnp.logical_and(off >= 0, off < PAIRS)
        return jnp.where(jnp.logical_and(inside, off == txt_at - PAIRS * v), 0.5, 0.0)

    row_part = (0.5 * jnp.exp(turned - row_lse) - same(j_at, i_at)).astype(BF16)
    col_part = (0.5 * jnp.exp(logits - col_lse) - same(i_at, j_at)).astype(BF16)
    for c in range(D // 256):
        cols = slice(c * 256, (c + 1) * 256)
        txt_c = mat_b[:, cols]
        img_c = mat_a[:, cols]
        whole_a[:, cols] = dot_tn(row_part, txt_c) + dot_nn(col_part, txt_c)
        whole_b[:, cols] = dot_nn(row_part, img_c) + dot_tn(col_part, img_c)
    diag = lax.broadcasted_iota(jnp.int32, (ROWS, 128), 0) == lax.broadcasted_iota(jnp.int32, (ROWS, 128), 1)
    for whole, mat, part, tell, say in (
            (whole_a, mat_a, part_a, tell_a, say_a), (whole_b, mat_b, part_b, tell_b, say_b)):
        along = jnp.zeros((ROWS, 128), F32)
        for c in range(CH):
            cols = slice(c * 128, (c + 1) * 128)
            along = along + whole[:, cols] * mat[:, cols].astype(F32)
        along = jnp.sum(along, 1, keepdims=True)
        for c in range(CH):
            cols = slice(c * 128, (c + 1) * 128)
            wide[pl.ds(c, ROWS, stride=CH), :] = whole[:, cols] - along * mat[:, cols].astype(F32)
        part[...] = wide[...].astype(BF16)
        row = jnp.sum(jnp.where(diag, along, 0.0), 0, keepdims=True)
        tell[...] = jnp.where(lane_at < ROWS, row, say)

    def piece(ref):
        return lambda slot: ref.at[pl.ds(pl.multiple_of(slot * SLOT, SLOT), SLOT)]

    third = exchange(
        2, piece(part_a), got_a.at[pl.ds(own_a, SLOT)], piece(part_b), got_b.at[pl.ds(own_b, SLOT)])
    notes = exchange(3, lambda slot: tell_a, note_a.at[u], lambda slot: tell_b, note_b.at[v])
    got_a[pl.ds(own_a, SLOT), :] = part_a[pl.ds(own_a, SLOT), :]
    got_b[pl.ds(own_b, SLOT), :] = part_b[pl.ds(own_b, SLOT), :]
    note_a[u] = tell_a[...]
    note_b[v] = tell_b[...]
    lax.fori_loop(2, PAIRS, grads, 0)
    for c in third:
        c.wait()
    for c in notes:
        c.wait()

    loss = jnp.zeros((1, 1), F32)
    for got, note, slot, unit, half, inv, out in (
            (got_a, note_a, u, img_unit, img_half, img_inv, gimg_out),
            (got_b, note_b, v, txt_unit, txt_half, txt_inv, gtxt_out)):
        total = got[0:SLOT, :].astype(F32)
        told = note[0]
        for k in range(1, GROUP):
            total = total + got[k * SLOT:(k + 1) * SLOT, :].astype(F32)
            told = told + note[k]
        loss = loss + told[:, ROWS:ROWS + 1]
        own = lane_at == PAIRS * slot + lax.broadcasted_iota(jnp.int32, (PAIRS, 128), 0)
        lead = jnp.sum(jnp.where(own, told, 0.0), 1, keepdims=True)
        stage[...] = total
        rows = [GLOBAL_SCALE * (stage[pl.ds(c, PAIRS, stride=CH), :]
                                + lead * half[:, c * 128:(c + 1) * 128].astype(F32)) for c in range(CH)]
        along = jnp.zeros((PAIRS, 1), F32)
        for c in range(CH):
            along = along + jnp.sum(rows[c] * unit[:, c * 128:(c + 1) * 128], 1, keepdims=True)
        for c in range(CH):
            cols = slice(c * 128, (c + 1) * 128)
            out[:, cols] = ((rows[c] - unit[:, cols] * along) * inv).astype(BF16)
    loss_out[...] = loss * (1.0 / (GROUP * GROUP * PAIRS))


def store_kernel(gtok_ref, gpat_ref, gimg_ref, gtxt_ref, loss_ref,
                 gtok_out, gpat_out, gimg_out, gtxt_out, loss_out, sem):
    copies = []
    for n in range(PAIRS):
        copies.append(pltpu.make_async_copy(gtok_ref.at[n], gtok_out.at[n], sem.at[0, n]))
        copies.append(pltpu.make_async_copy(gpat_ref.at[n], gpat_out.at[n], sem.at[1, n]))
    for c in copies:
        c.start()
    gimg_out[...] = gimg_ref[...]
    gtxt_out[...] = gtxt_ref[...]
    loss_out[...] = loss_ref[...]
    for c in copies:
        c.wait()


def body(tokens, patches, lengths, img_pooled, txt_pooled):
    vmem = pl.BlockSpec(memory_space=pltpu.VMEM)
    hbm = pl.BlockSpec(memory_space=pltpu.HBM)
    sds = jax.ShapeDtypeStruct
    vm = pltpu.VMEM
    square = (PAIRS, T, T)
    gtok, gpat, gimg, gtxt, loss = pl.pallas_call(
        exchange_kernel,
        name="exchange",
        out_shape=(
            vm((PAIRS, T, D), BF16), vm((PAIRS, T, D), BF16),
            vm((PAIRS, D), BF16), vm((PAIRS, D), BF16), vm((1, 1), F32)),
        in_specs=[hbm] * 5,
        out_specs=(vmem,) * 5,
        scratch_shapes=[
            vm((PAIRS, T, D), BF16), vm((PAIRS, T, D), BF16),
            vm(square, F32), vm(square, BF16), vm(square, BF16), vm(square, BF16), vm(square, F32),
            vm((T, T), F32), vm((T, T), F32), vm(square, BF16), vm((T, T), BF16), vm(square, BF16),
            vm((PAIRS, 8, T), F32), vm((PAIRS, T, 128), BF16),
            vm((SLOT, 128), F32), vm((GROUP * SLOT, 128), BF16), vm((GROUP * SLOT, 128), BF16),
            vm((ROWS, D), BF16), vm((ROWS, D), BF16), vm((GROUP * SLOT, 128), F32),
            vm((SLOT, 128), BF16), vm((SLOT, 128), BF16),
            vm((GROUP * SLOT, 128), BF16), vm((GROUP * SLOT, 128), BF16),
            vm((ROWS, D), F32), vm((ROWS, D), F32),
            vm((GROUP, 4, 128), F32), vm((GROUP, 4, 128), F32),
            vm((GROUP * SLOT, 128), BF16), vm((GROUP * SLOT, 128), BF16),
            vm((GROUP, 1, 128), F32), vm((GROUP, 1, 128), F32), vm((1, 128), F32), vm((1, 128), F32),
            vm((8, 128), F32), pltpu.SMEM((PAIRS,), jnp.int32), vm((PAIRS, D), BF16), vm((PAIRS, D), BF16),
            pltpu.SemaphoreType.DMA((2, PAIRS)), pltpu.SemaphoreType.DMA((3,)),
            pltpu.SemaphoreType.DMA((4, 2, GROUP - 1)),
            pltpu.SemaphoreType.DMA((4, 2, GROUP - 1)),
        ],
        compiler_params=pltpu.CompilerParams(
            collective_id=0, has_side_effects=True, vmem_limit_bytes=40 << 20),
    )(*(pltpu.with_memory_space_constraint(a, pltpu.HBM)
        for a in (lengths, tokens, patches, img_pooled, txt_pooled)))

    gtok, gpat, gimg, gtxt, loss = pl.pallas_call(
        store_kernel,
        name="store",
        out_shape=(
            sds((PAIRS, T, D), BF16), sds((PAIRS, T, D), BF16),
            sds((PAIRS, D), BF16), sds((PAIRS, D), BF16), sds((1, 1), F32)),
        in_specs=[vmem] * 5,
        out_specs=(hbm, hbm, vmem, vmem, vmem),
        scratch_shapes=[pltpu.SemaphoreType.DMA((2, PAIRS))],
        compiler_params=pltpu.CompilerParams(vmem_limit_bytes=32 << 20),
    )(gtok, gpat, gimg, gtxt, loss)
    return gtok, gpat, gimg, gtxt, loss.reshape(())


def solution(mesh):
    both = ("dp", "grp")
    placed = (P(both, None, None), P(both, None, None), P(both), P(both, None), P(both, None))
    return jax.shard_map(
        body,
        mesh=mesh,
        in_specs=placed,
        out_specs=(P(both, None, None), P(both, None, None), P(both, None), P(both, None), P()),
        check_vma=False,
    )
```

time: 48.6 us -> 34.8 us (0.72)
  Pallas kernels: 43.1 us -> 34 us
  local copies, waits for them, and re-layouts: 4.52 us -> 0 us
    pallas_call x2, Pallas kernels: 43.1 us -> 34 us  [the longest x1 30.7 us: body(): pl.pallas_call(exchange_kernel, name='exchange', out_shape=(vm((PAIRS, T,...]
    unnamed x14 -> x0, local copies, waits for them, and re-layouts: 4.52 us -> none
where the time goes in v2:
time: 34.8 us; the launch traced here: 34.7 us
  Pallas kernels  34 us (98%)
  between operations  0.64 us (2%)
    pallas_call x1, Pallas kernels, body(): pl.pallas_call(exchange_kernel, name='exchange', out_shape=(vm((PAIRS, T,...  30.7 us
    pallas_call x1, Pallas kernels, body(): pl.pallas_call(store_kernel, name='store', out_shape=(sds((PAIRS, T, D),...  3.31 us

profile of v2, /device:TPU:1, one launch (start us, length us, event | category | flops | bytes accessed | tf_op | source)
XLA Modules:
  0.0 34.7 jit_solution(8825315455155446794)
XLA Ops:
  0.6 30.7 %exchange.1 = (bf16[4,256,1024]{2,1,0:T(8,128)(2,1)S(1)}, bf16[4,256,1024]{2,1,0:T(8,128)(2,1)S(1)}, bf16[4,1024]{1,0:T(4,128)(2,1)S(1)}, bf16[4,1024]{1,0:T(4,128)(2,1)S(1)}, f32[1,1]{1,0:T(1,128)}) custom-call(s32[4]{0:T(128)} %len_hbm.1, bf16[4,256,1024]{2,1,0:T(8,128)(2,1)} %tok_hbm.1, bf16[4,256,1024]{2,1,0:T(8,128)(2,1)} %pat_hbm.1, ...), custom_call_target="tpu_custom_call" | custom-call | tf_op jit(solution)/shard_map/exchange/pallas_call | solution.py:406
  31.4 3.3 %store.1 = (bf16[4,256,1024]{2,1,0:T(8,128)(2,1)}, bf16[4,256,1024]{2,1,0:T(8,128)(2,1)}, bf16[4,1024]{1,0:T(4,128)(2,1)}, bf16[4,1024]{1,0:T(4,128)(2,1)}, f32[1,1]{1,0:T(1,128)}) custom-call(bf16[4,256,1024]{2,1,0:T(8,128)(2,1)S(1)} %get-tuple-element.15.gtok_ref, bf16[4,256,1024]{2,1,0:T(8,128)(2,1)S(1)} %get-tuple-element.16.gpat_ref, ...), custom_call_target="tpu_custom_call" | custom-call | tf_op jit(solution)/shard_map/store/pallas_call | solution.py:437

commit v3 on v2

--- a/solution.py
+++ b/solution.py
@@ -205,32 +205,31 @@
         ((len_hbm, len_ref), (img_hbm, img_ref), (txt_hbm, txt_ref)))]
     for c in small:
         c.start()
-    loads = []
-    for n in range(PAIRS):
-        loads.append((
-            pltpu.make_async_copy(tok_hbm.at[n], tok_v.at[n], in_sem.at[0, n]),
-            pltpu.make_async_copy(pat_hbm.at[n], pat_v.at[n], in_sem.at[1, n]),
-        ))
-        loads[-1][0].start()
-        loads[-1][1].start()
-
+    def load(n):
+        pltpu.make_async_copy(tok_hbm.at[n], tok_v.at[n], in_sem.at[0, n]).start()
+        pltpu.make_async_copy(pat_hbm.at[n], pat_v.at[n], in_sem.at[1, n]).start()
+
+    load(0)
     barrier = pltpu.get_barrier_semaphore()
     for (dev_a, _), (dev_b, _) in zip(peers_a, peers_b):
         pl.semaphore_signal(barrier, inc=1, device_id=dev_a, device_id_type=MESH)
         pl.semaphore_signal(barrier, inc=1, device_id=dev_b, device_id_type=MESH)
 
-    def exchange(phase, src_a, dst_a, src_b, dst_b):
-        copies = []
-        for k in range(GROUP - 1):
-            for side, peers, src, dst in ((0, peers_a, src_a, dst_a), (1, peers_b, src_b, dst_b)):
-                dev, slot = peers[k]
-                copies.append(pltpu.make_async_remote_copy(
-                    src_ref=src(slot), dst_ref=dst,
-                    send_sem=send_sem.at[phase, side, k], recv_sem=recv_sem.at[phase, side, k],
-                    device_id=dev, device_id_type=MESH))
-        for c in copies:
-            c.start()
-        return copies
+    def exchange(phase, side, peers, src, dst):
+        for dev, slot in peers:
+            pltpu.make_async_remote_copy(
+                src_ref=src(slot), dst_ref=dst,
+                send_sem=send_sem.at[phase, side], recv_sem=recv_sem.at[phase, side],
+                device_id=dev, device_id_type=MESH).start()
+
+    def arrived(phase, side, many):
+        pltpu.make_async_copy(many, many, recv_sem.at[phase, side]).wait()
+
+    def sent(phase, side, many):
+        pltpu.make_async_copy(many, many, send_sem.at[phase, side]).wait()
+
+    peer_rows = pl.ds(0, (GROUP - 1) * SLOT)
+    peer_slots = pl.ds(0, GROUP - 1)
 
     for c in small:
         c.wait()
@@ -258,21 +257,23 @@
                    gtok_out, gpat_out)
         return carry
 
-    fine_ref[...] = jnp.zeros_like(fine_ref)
-    lax.fori_loop(0, 1, losses, 0)
-    pl.semaphore_wait(barrier, 2 * (GROUP - 1))
-
     own_a = pl.multiple_of(u * SLOT, SLOT)
     own_b = pl.multiple_of(v * SLOT, SLOT)
-    first = exchange(
-        0, lambda slot: half_a, unit_a.at[pl.ds(own_a, SLOT)],
-        lambda slot: half_b, unit_b.at[pl.ds(own_b, SLOT)])
+    fine_ref[...] = jnp.zeros_like(fine_ref)
     unit_a[pl.ds(own_a, SLOT), :] = half_a[...]
     unit_b[pl.ds(own_b, SLOT), :] = half_b[...]
 
-    lax.fori_loop(1, PAIRS, losses, 0)
-    for c in first:
-        c.wait()
+    def load_next(n, carry):
+        load(n)
+        return carry
+
+    lax.fori_loop(1, PAIRS, load_next, 0)
+    pl.semaphore_wait(barrier, 2 * (GROUP - 1))
+    exchange(0, 1, peers_b, lambda slot: half_b, unit_b.at[pl.ds(own_b, SLOT)])
+    exchange(0, 0, peers_a, lambda slot: half_a, unit_a.at[pl.ds(own_a, SLOT)])
+    lax.fori_loop(0, PAIRS, losses, 0)
+    arrived(0, 0, unit_a.at[peer_rows])
+    arrived(0, 1, unit_b.at[peer_rows])
 
     for src, dst in ((unit_a, mat_a), (unit_b, mat_b)):
         wide[...] = src[...].astype(F32)
@@ -287,11 +288,11 @@
         dst[row, 0:1, 0:ROWS] = top
         dst[row, 1:2, 0:ROWS] = jnp.sum(jnp.exp(block - top), 0, keepdims=True)
         dst[row, 2:3, :] = jnp.broadcast_to(scalar, (1, 128))
-    second = exchange(
-        1, lambda slot: stat_a.at[u], stat_a.at[u], lambda slot: stat_b.at[v], stat_b.at[v])
+    exchange(1, 1, peers_b, lambda slot: stat_b.at[v], stat_b.at[v])
+    exchange(1, 0, peers_a, lambda slot: stat_a.at[u], stat_a.at[u])
     lax.fori_loop(0, 2, grads, 0)
-    for c in second:
-        c.wait()
+    arrived(1, 0, stat_a.at[peer_slots])
+    arrived(1, 1, stat_b.at[peer_slots])
 
     def combine(stat):
         top = stat[0, 0:1, 0:ROWS]
@@ -321,15 +322,19 @@
 
     row_part = (0.5 * jnp.exp(turned - row_lse) - same(j_at, i_at)).astype(BF16)
     col_part = (0.5 * jnp.exp(logits - col_lse) - same(i_at, j_at)).astype(BF16)
-    for c in range(D // 256):
-        cols = slice(c * 256, (c + 1) * 256)
-        txt_c = mat_b[:, cols]
-        img_c = mat_a[:, cols]
-        whole_a[:, cols] = dot_tn(row_part, txt_c) + dot_nn(col_part, txt_c)
-        whole_b[:, cols] = dot_nn(row_part, img_c) + dot_tn(col_part, img_c)
     diag = lax.broadcasted_iota(jnp.int32, (ROWS, 128), 0) == lax.broadcasted_iota(jnp.int32, (ROWS, 128), 1)
-    for whole, mat, part, tell, say in (
-            (whole_a, mat_a, part_a, tell_a, say_a), (whole_b, mat_b, part_b, tell_b, say_b)):
+
+    def piece(ref):
+        return lambda slot: ref.at[pl.ds(pl.multiple_of(slot * SLOT, SLOT), SLOT)]
+
+    def partials(other, mat, whole, part, tell, say, turn):
+        for c in range(D // 256):
+            cols = slice(c * 256, (c + 1) * 256)
+            far = other[:, cols]
+            if turn:
+                whole[:, cols] = dot_tn(row_part, far) + dot_nn(col_part, far)
+            else:
+                whole[:, cols] = dot_nn(row_part, far) + dot_tn(col_part, far)
         along = jnp.zeros((ROWS, 128), F32)
         for c in range(CH):
             cols = slice(c * 128, (c + 1) * 128)
@@ -342,21 +347,24 @@
         row = jnp.sum(jnp.where(diag, along, 0.0), 0, keepdims=True)
         tell[...] = jnp.where(lane_at < ROWS, row, say)
 
-    def piece(ref):
-        return lambda slot: ref.at[pl.ds(pl.multiple_of(slot * SLOT, SLOT), SLOT)]
-
-    third = exchange(
-        2, piece(part_a), got_a.at[pl.ds(own_a, SLOT)], piece(part_b), got_b.at[pl.ds(own_b, SLOT)])
-    notes = exchange(3, lambda slot: tell_a, note_a.at[u], lambda slot: tell_b, note_b.at[v])
+    partials(mat_a, mat_b, whole_b, part_b, tell_b, say_b, False)
+    partials(mat_b, mat_a, whole_a, part_a, tell_a, say_a, True)
     got_a[pl.ds(own_a, SLOT), :] = part_a[pl.ds(own_a, SLOT), :]
     got_b[pl.ds(own_b, SLOT), :] = part_b[pl.ds(own_b, SLOT), :]
     note_a[u] = tell_a[...]
     note_b[v] = tell_b[...]
+    exchange(2, 1, peers_b, piece(part_b), got_b.at[pl.ds(own_b, SLOT)])
+    exchange(2, 0, peers_a, piece(part_a), got_a.at[pl.ds(own_a, SLOT)])
+    exchange(3, 1, peers_b, lambda _: tell_b, note_b.at[v])
+    exchange(3, 0, peers_a, lambda _: tell_a, note_a.at[u])
     lax.fori_loop(2, PAIRS, grads, 0)
-    for c in third:
-        c.wait()
-    for c in notes:
-        c.wait()
+    for side, unit, stat, got, note in ((0, unit_a, stat_a, got_a, note_a), (1, unit_b, stat_b, got_b, note_b)):
+        sent(0, side, unit.at[peer_rows])
+        sent(1, side, stat.at[peer_slots])
+        sent(2, side, got.at[peer_rows])
+        sent(3, side, note.at[peer_slots])
+        arrived(2, side, got.at[peer_rows])
+        arrived(3, side, note.at[peer_slots])
 
     loss = jnp.zeros((1, 1), F32)
     for got, note, slot, unit, half, inv, out in (
@@ -379,20 +387,21 @@
         for c in range(CH):
             cols = slice(c * 128, (c + 1) * 128)
             out[:, cols] = ((rows[c] - unit[:, cols] * along) * inv).astype(BF16)
-    loss_out[...] = loss * (1.0 / (GROUP * GROUP * PAIRS))
+    loss_out[...] = jnp.broadcast_to(loss * (1.0 / (GROUP * GROUP * PAIRS)), loss_out.shape)
 
 
 def store_kernel(gtok_ref, gpat_ref, gimg_ref, gtxt_ref, loss_ref,
-                 gtok_out, gpat_out, gimg_out, gtxt_out, loss_out, sem):
+                 gtok_out, gpat_out, gimg_out, gtxt_out, loss_out, one, sem):
     copies = []
     for n in range(PAIRS):
         copies.append(pltpu.make_async_copy(gtok_ref.at[n], gtok_out.at[n], sem.at[0, n]))
         copies.append(pltpu.make_async_copy(gpat_ref.at[n], gpat_out.at[n], sem.at[1, n]))
+    copies.append(pltpu.make_async_copy(gimg_ref, gimg_out, sem.at[2, 0]))
+    copies.append(pltpu.make_async_copy(gtxt_ref, gtxt_out, sem.at[2, 1]))
+    copies.append(pltpu.make_async_copy(one, loss_out, sem.at[2, 2]))
+    one[...] = loss_ref[0:1, 0:1]
     for c in copies:
         c.start()
-    gimg_out[...] = gimg_ref[...]
-    gtxt_out[...] = gtxt_ref[...]
-    loss_out[...] = loss_ref[...]
     for c in copies:
         c.wait()
 
@@ -408,7 +417,7 @@
         name="exchange",
         out_shape=(
             vm((PAIRS, T, D), BF16), vm((PAIRS, T, D), BF16),
-            vm((PAIRS, D), BF16), vm((PAIRS, D), BF16), vm((1, 1), F32)),
+            vm((PAIRS, D), BF16), vm((PAIRS, D), BF16), vm((8, 128), F32)),
         in_specs=[hbm] * 5,
         out_specs=(vmem,) * 5,
         scratch_shapes=[
@@ -426,8 +435,8 @@
             vm((GROUP, 1, 128), F32), vm((GROUP, 1, 128), F32), vm((1, 128), F32), vm((1, 128), F32),
             vm((8, 128), F32), pltpu.SMEM((PAIRS,), jnp.int32), vm((PAIRS, D), BF16), vm((PAIRS, D), BF16),
             pltpu.SemaphoreType.DMA((2, PAIRS)), pltpu.SemaphoreType.DMA((3,)),
-            pltpu.SemaphoreType.DMA((4, 2, GROUP - 1)),
-            pltpu.SemaphoreType.DMA((4, 2, GROUP - 1)),
+            pltpu.SemaphoreType.DMA((4, 2)),
+            pltpu.SemaphoreType.DMA((4, 2)),
         ],
         compiler_params=pltpu.CompilerParams(
             collective_id=0, has_side_effects=True, vmem_limit_bytes=40 << 20),
@@ -441,8 +450,8 @@
             sds((PAIRS, T, D), BF16), sds((PAIRS, T, D), BF16),
             sds((PAIRS, D), BF16), sds((PAIRS, D), BF16), sds((1, 1), F32)),
         in_specs=[vmem] * 5,
-        out_specs=(hbm, hbm, vmem, vmem, vmem),
-        scratch_shapes=[pltpu.SemaphoreType.DMA((2, PAIRS))],
+        out_specs=(hbm,) * 5,
+        scratch_shapes=[vm((1, 1), F32), pltpu.SemaphoreType.DMA((3, PAIRS))],
         compiler_params=pltpu.CompilerParams(vmem_limit_bytes=32 << 20),
     )(gtok, gpat, gimg, gtxt, loss)
     return gtok, gpat, gimg, gtxt, loss.reshape(())

time: 34.8 us -> 30.7 us (0.88)
  Pallas kernels: 34 us -> 30 us
    pallas_call x1, Pallas kernels: 30.7 us -> 27.8 us  [body(): pl.pallas_call(exchange_kernel, name='exchange', out_shape=(vm((PAIRS, T,...]
    pallas_call x1, Pallas kernels: 3.31 us -> 2.11 us  [body(): pl.pallas_call(store_kernel, name='store', out_shape=(sds((PAIRS, T, D),...]
where the time goes in v3:
time: 30.7 us; the launch traced here: 30.6 us
  Pallas kernels  30 us (98%)
  between operations  0.64 us (2%)
    pallas_call x1, Pallas kernels, body(): pl.pallas_call(exchange_kernel, name='exchange', out_shape=(vm((PAIRS, T,...  27.8 us
    pallas_call x1, Pallas kernels, body(): pl.pallas_call(store_kernel, name='store', out_shape=(sds((PAIRS, T, D),...  2.11 us

profile of v3, /device:TPU:1, one launch (start us, length us, event | category | flops | bytes accessed | tf_op | source)
XLA Modules:
  0.0 30.6 jit_solution(16539156694985457522)
XLA Ops:
  0.6 27.8 %exchange.1 = (bf16[4,256,1024]{2,1,0:T(8,128)(2,1)S(1)}, bf16[4,256,1024]{2,1,0:T(8,128)(2,1)S(1)}, bf16[4,1024]{1,0:T(4,128)(2,1)S(1)}, bf16[4,1024]{1,0:T(4,128)(2,1)S(1)}, f32[8,128]{1,0:T(8,128)S(1)}) custom-call(s32[4]{0:T(128)} %len_hbm.1, bf16[4,256,1024]{2,1,0:T(8,128)(2,1)} %tok_hbm.1, bf16[4,256,1024]{2,1,0:T(8,128)(2,1)} %pat_hbm.1, ...), custom_call_target="tpu_custom_call" | custom-call | tf_op jit(solution)/shard_map/exchange/pallas_call | solution.py:415
  28.5 2.1 %store.1 = (bf16[4,256,1024]{2,1,0:T(8,128)(2,1)}, bf16[4,256,1024]{2,1,0:T(8,128)(2,1)}, bf16[4,1024]{1,0:T(4,128)(2,1)}, bf16[4,1024]{1,0:T(4,128)(2,1)}, f32[1,1]{1,0:T(1,128)}) custom-call(bf16[4,256,1024]{2,1,0:T(8,128)(2,1)S(1)} %get-tuple-element.15.gtok_ref, bf16[4,256,1024]{2,1,0:T(8,128)(2,1)S(1)} %get-tuple-element.16.gpat_ref, ...), custom_call_target="tpu_custom_call" | custom-call | tf_op jit(solution)/shard_map/store/pallas_call | solution.py:446
